TPU v7x, 512 devices: a whole 4x8x8 slice. The times are simulated.
512 devices in a mesh: req: 8 (over y), seq: 8 (over x, core), tp: 8 (over z).
Axes of the slice: x: 4, y: 8, z: 8, core: 2. Of those that a mesh axis runs over, the one named last changes fastest.
Arguments:
- tokens: bfloat16 [2048, 1024], P(('req', 'seq', 'tp')), may hold values from -3 to 3
- w_qkv: bfloat16 [1024, 3, 1024], P(None, None, 'tp'), may hold values from -0.1875 to 0.1875
- w_out: bfloat16 [1024, 1024], P('tp'), may hold values from -0.75 to 0.75
- variate_bias: float32 [2, 16], P(None, 'tp'), may hold values from -2 to 2
- attn_gain: float32 [1024], replicated, may hold values from 0.25 to 1.75
- ffn_gain: float32 [1024], replicated, may hold values from 0.25 to 1.75
- gate_up: bfloat16 [1024, 64, 128], P(None, ('seq', 'tp')), may hold values from -0.1875 to 0.1875
- w_down: bfloat16 [64, 64, 1024], P(('seq', 'tp')), may hold values from -0.09375 to 0.09375
- cache_keys: bfloat16 [1536, 256, 1024], P(('req', 'seq'), None, 'tp'), may hold values from -360 to 360
- cache_values: bfloat16 [1536, 256, 1024], P(('req', 'seq'), None, 'tp'), may hold values from -6 to 6
- cache_variate: int32 [1536, 256], P(('req', 'seq')), may hold values from 0 to 3
- new_variate: int32 [512, 4], P('req'), may hold values from 0 to 3
- piece_slot: int32 [512, 64], P('req'), may hold values from -1 to 191, as said below
- cache_len: int32 [512], P('req'), may hold values from 1 to 16384, as said below
Outputs:
- layer_out: bfloat16 [2048, 1024], P(('req', 'seq', 'tp'))
Inputs may be any that keep to these rules, and one draw needn't show every extreme that they name: `cache_len`: in each aligned block of 64 requests exactly one request has the most cached positions. `piece_slot`: entry p of request r is the slot within its group that holds cache positions p * 256 to p * 256 + 255; it is -1 exactly when p * 256 >= cache_len[r]; no slot of a group holds two pieces; slots that hold no piece are never read.
All inputs are finite; a program needn't handle non-finite values.
Results may differ from a plain program's by a relative error of at most 0.022.
Values may be sent and summed in bfloat16 or wider, within the bound.
No kernel may reach another device: no remote copies, remote signals or barrier semaphores. Data moves between devices by JAX's collectives and lax.ppermute only.
A program may use at most 64 MiB of HBM per device.

v0:
```python
import math
import jax
import jax.numpy as jnp
from jax import lax
from jax.sharding import PartitionSpec as P

HD = 64
EPSILON = 1e-05
MASKED_SCORE = -1e30


def joined(value, axis, combine):
    everything = jax.tree.map(lambda part: lax.all_gather(part, axis), value)
    first = jax.tree.map(lambda part: part[0], everything)

    def step(k, so_far):
        return combine(so_far, jax.tree.map(lambda part: part[k], everything))

    return lax.fori_loop(1, lax.axis_size(axis), step, first)


def rms_scale(rows, gain):
    rows32 = rows.astype(jnp.float32)
    mean_sq = jnp.mean(rows32 * rows32, axis=-1, keepdims=True)
    return (rows32 * lax.rsqrt(mean_sq + EPSILON) * gain).astype(jnp.bfloat16)


def rotate(vectors, positions):
    half_size = vectors.shape[-1] // 2
    inv_freq = 10000.0 ** (-jnp.arange(half_size, dtype=jnp.float32) / half_size)
    angles = positions[:, None] * inv_freq[None, :]
    cosine = jnp.cos(angles)[:, None, :]
    sine_part = jnp.sin(angles)[:, None, :]
    earlier = vectors[..., :half_size]
    latter = vectors[..., half_size:]
    return jnp.concatenate(
        [earlier * cosine - latter * sine_part, latter * cosine + earlier * sine_part], axis=-1
    )


def row_positions(lengths, step_count):
    offsets = jnp.arange(step_count, dtype=jnp.int32)
    return (lengths[:, None] + offsets[None, :]).reshape(-1).astype(jnp.float32)


def split_heads(projected, positions, head_size):
    row_count = projected.shape[0]
    parts = projected.reshape(row_count, 3, -1, head_size)
    queries = rotate(parts[:, 0], positions).astype(jnp.bfloat16)
    keys_new = rotate(parts[:, 1], positions).astype(jnp.bfloat16)
    values_new = parts[:, 2].astype(jnp.bfloat16)
    return (queries, keys_new, values_new)


def cache_partials(
    queries,
    cache_keys,
    cache_values,
    cache_variate,
    new_variate,
    piece_slot,
    cache_len,
    variate_bias,
    score_scale,
):
    slot_count, piece_len, _ = cache_keys.shape
    requests, step_count, heads, head_size = queries.shape
    max_pieces = piece_slot.shape[1]
    slot_ids = lax.axis_index("seq") * slot_count + jnp.arange(slot_count, dtype=jnp.int32)
    matches = piece_slot[None, :, :] == slot_ids[:, None, None]
    owners = jnp.any(matches, axis=2)
    piece_index = jnp.sum(
        jnp.where(matches, jnp.arange(max_pieces, dtype=jnp.int32)[None, None, :], 0), axis=(1, 2)
    )
    owner_len = jnp.sum(jnp.where(owners, cache_len[None, :], 0), axis=1)
    positions_in = (
        piece_index[:, None] * piece_len + jnp.arange(piece_len, dtype=jnp.int32)[None, :]
    )
    is_valid = positions_in < owner_len[:, None]
    picker = owners.astype(jnp.bfloat16)
    slot_query = jnp.dot(
        picker, queries.reshape(requests, -1), preferred_element_type=jnp.float32
    ).astype(jnp.bfloat16)
    slot_query = slot_query.reshape(slot_count, step_count, heads, head_size)
    slot_variate = jnp.sum(jnp.where(owners[:, :, None], new_variate[None], 0), axis=1)
    same_var = slot_variate[:, :, None] == cache_variate[:, None, :]
    bias_terms = jnp.where(
        same_var[:, None],
        variate_bias[0][None, :, None, None],
        variate_bias[1][None, :, None, None],
    )
    key_rows = cache_keys.reshape(slot_count, piece_len, heads, head_size)
    value_rows = cache_values.reshape(slot_count, piece_len, heads, head_size)
    scores = (
        jnp.einsum("sthd,slhd->shtl", slot_query, key_rows, preferred_element_type=jnp.float32)
        * score_scale
        + bias_terms
    )
    scores = jnp.where(is_valid[:, None, None, :], scores, MASKED_SCORE)
    slot_top = jnp.max(scores, axis=3)
    weights = jnp.where(is_valid[:, None, None, :], jnp.exp(scores - slot_top[..., None]), 0.0)
    slot_total = jnp.sum(weights, axis=3)
    slot_out = jnp.einsum(
        "shtl,slhd->shtd",
        weights.astype(jnp.bfloat16),
        value_rows,
        preferred_element_type=jnp.float32,
    )
    top_cache = jnp.max(
        jnp.where(owners[:, :, None, None], slot_top[:, None], MASKED_SCORE), axis=0
    )
    top_at = jnp.sum(jnp.where(owners[:, :, None, None], top_cache[None], 0.0), axis=1)
    factor = jnp.exp(slot_top - top_at)
    owner_f = owners.astype(jnp.float32)
    cache_total = jnp.einsum(
        "sr,sht->rht", owner_f, slot_total * factor, precision=lax.Precision.HIGHEST
    )
    cache_out = jnp.einsum(
        "sr,shtd->rhtd", owner_f, slot_out * factor[..., None], precision=lax.Precision.HIGHEST
    )
    return (top_cache, cache_total, cache_out)


def merge_pair(earlier, latter):
    joint_top = jnp.maximum(earlier[0], latter[0])
    left_scale = jnp.exp(earlier[0] - joint_top)
    right_scale = jnp.exp(latter[0] - joint_top)
    joint_total = earlier[1] * left_scale + latter[1] * right_scale
    joint_out = earlier[2] * left_scale[..., None] + latter[2] * right_scale[..., None]
    return (joint_top, joint_total, joint_out)


def finish(
    top_cache,
    cache_total,
    cache_out,
    queries,
    keys_new,
    values_new,
    new_variate,
    variate_bias,
    score_scale,
):
    step_count = new_variate.shape[1]
    new_scores = (
        jnp.einsum("rthd,ruhd->rhtu", queries, keys_new, preferred_element_type=jnp.float32)
        * score_scale
    )
    same_var = new_variate[:, :, None] == new_variate[:, None, :]
    new_scores = new_scores + jnp.where(
        same_var[:, None],
        variate_bias[0][None, :, None, None],
        variate_bias[1][None, :, None, None],
    )
    step_ids = jnp.arange(step_count, dtype=jnp.int32)
    causal = step_ids[:, None] >= step_ids[None, :]
    new_scores = jnp.where(causal[None, None], new_scores, MASKED_SCORE)
    row_top = jnp.maximum(top_cache, jnp.max(new_scores, axis=3))
    new_weights = jnp.where(causal[None, None], jnp.exp(new_scores - row_top[..., None]), 0.0)
    carried = jnp.exp(top_cache - row_top)
    row_total = cache_total * carried + jnp.sum(new_weights, axis=3)
    mixed_out = cache_out * carried[..., None] + jnp.einsum(
        "rhtu,ruhd->rhtd",
        new_weights.astype(jnp.bfloat16),
        values_new,
        preferred_element_type=jnp.float32,
    )
    attended = mixed_out / row_total[..., None]
    requests, heads, _, head_size = attended.shape
    return (
        jnp.transpose(attended, (0, 2, 1, 3))
        .reshape(requests * step_count, heads * head_size)
        .astype(jnp.bfloat16)
    )


def make_expand(gate_blocks, unit_block, row_block):
    block_count = gate_blocks.shape[1]
    expanded = jnp.einsum("nd,dbu->nbu", row_block, gate_blocks, preferred_element_type=jnp.float32)
    gate_part = expanded[:, :, :unit_block]
    up_part = expanded[:, :, unit_block:]
    return (
        (jax.nn.silu(gate_part) * up_part)
        .astype(jnp.bfloat16)
        .reshape(row_block.shape[0], block_count * unit_block)
    )


def on_device(
    tokens,
    w_qkv,
    w_out,
    variate_bias,
    attn_gain,
    ffn_gain,
    gate_up,
    w_down,
    cache_keys,
    cache_values,
    cache_variate,
    new_variate,
    piece_slot,
    cache_len,
):
    row_count = tokens.shape[0]
    requests, step_count = new_variate.shape
    score_scale = 1.0 / math.sqrt(HD)
    normed = rms_scale(tokens, attn_gain)
    qkv_width = w_qkv.shape[2]
    flat_qkv = w_qkv.reshape(w_qkv.shape[0], 3 * qkv_width)
    projected = jnp.dot(
        lax.all_gather(normed, ("seq", "tp"), axis=0, tiled=True),
        flat_qkv,
        preferred_element_type=jnp.float32,
    )
    queries, keys_new, values_new = split_heads(projected, row_positions(cache_len, step_count), HD)
    shape_four = (requests, step_count, qkv_width // HD, HD)
    queries = queries.reshape(shape_four)
    keys_new = keys_new.reshape(shape_four)
    values_new = values_new.reshape(shape_four)
    top_cache, cache_total, cache_out = cache_partials(
        queries,
        cache_keys,
        cache_values,
        cache_variate,
        new_variate,
        piece_slot,
        cache_len,
        variate_bias,
        score_scale,
    )
    top_cache, cache_total, cache_out = joined(
        (top_cache, cache_total, cache_out), "seq", merge_pair
    )
    attended = finish(
        top_cache,
        cache_total,
        cache_out,
        queries,
        keys_new,
        values_new,
        new_variate,
        variate_bias,
        score_scale,
    )
    seq_base = lax.axis_index("seq") * (row_count * lax.axis_size("tp"))
    picked = lax.dynamic_slice_in_dim(attended, seq_base, row_count * lax.axis_size("tp"), 0)
    attn_rows_sum = lax.psum_scatter(
        jnp.dot(picked, w_out, preferred_element_type=jnp.float32).astype(jnp.bfloat16),
        "tp",
        scatter_dimension=0,
        tiled=True,
    ).astype(jnp.float32)
    mid = tokens.astype(jnp.float32) + attn_rows_sum
    normed_mid = rms_scale(mid, ffn_gain)
    unit_block = w_down.shape[1]
    model_width = w_down.shape[2]
    hidden = make_expand(
        gate_up, unit_block, lax.all_gather(normed_mid, ("seq", "tp"), axis=0, tiled=True)
    )
    flat_down = w_down.reshape(w_down.shape[0] * unit_block, model_width)
    picked = hidden
    ffn_rows_sum = lax.psum_scatter(
        jnp.dot(picked, flat_down, preferred_element_type=jnp.float32),
        ("seq", "tp"),
        scatter_dimension=0,
        tiled=True,
    )
    return (mid + ffn_rows_sum).astype(jnp.bfloat16)


def solution(mesh):
    in_specs = (
        P(("req", "seq", "tp"), None),
        P(None, None, "tp"),
        P("tp", None),
        P(None, "tp"),
        P(),
        P(),
        P(None, ("seq", "tp"), None),
        P(("seq", "tp"), None, None),
        P(("req", "seq"), None, "tp"),
        P(("req", "seq"), None, "tp"),
        P(("req", "seq"), None),
        P("req", None),
        P("req", None),
        P("req"),
    )
    out_specs = P(("req", "seq", "tp"), None)
    return jax.shard_map(
        on_device, mesh=mesh, in_specs=in_specs, out_specs=out_specs, check_vma=False
    )
```

profile of v0, /device:TPU:8, one launch (start us, length us, event | category | flops | bytes accessed | tf_op | source)
XLA Modules:
  0.0 463.1 jit_solution(17933760203444792327)
XLA Ops:
  6.6 1.4 fusion.9
  8.0 1.3 compare_reduce_fusion
  9.9 0.8 fusion.31
  10.8 1.3 slice_bitcast_fusion.3
  12.8 1.3 select_reduce_fusion.3
  14.1 0.8 select_reduce_fusion.2
  16.5 55.1 %all-gather.3 = bf16[64,4,1024]{2,1,0:T(4,128)(2,1)S(1)} all-gather(bf16[1,4,1024]{2,1,0:T(4,128)(2,1)S(1)} %fusion.39), channel_id=1, replica_groups=mesh['req'=8,'seq'=8,'tp'=8] {'seq','tp'}, dimensions={0}, use_global_device_ids=true | all-gather | bytes 532480 | tf_op jit(solution)/shard_map/all_gather | solution.py:212
  75.4 0.9 broadcast_compare_fusion
  76.4 1.7 fusion.47
  78.3 1.2 fusion.20
  80.5 1.5 convolution_multiply_fusion.1
  82.0 1.0 fusion.22
  83.1 0.9 slice.97
  85.9 13.5 %all-gather = f32[512,2,4]{2,1,0:T(2,128)S(1)} all-gather(f32[64,2,4]{2,1,0:T(2,128)S(1)} %copy.150), channel_id=2, replica_groups=mesh['req'=8,'seq'=8,'tp'=8] {'seq'}, dimensions={0}, use_global_device_ids=true | all-gather | bytes 18432 | tf_op jit(solution)/shard_map/all_gather | solution.py:13
  99.7 13.6 %all-gather.1 = f32[512,2,4]{2,1,0:T(2,128)S(1)} all-gather(f32[64,2,4]{2,1,0:T(2,128)S(1)} %copy.153), channel_id=3, replica_groups=mesh['req'=8,'seq'=8,'tp'=8] {'seq'}, dimensions={0}, use_global_device_ids=true | all-gather | bytes 18432 | tf_op jit(solution)/shard_map/all_gather | solution.py:13
  113.8 1.0 slice.67
  114.9 14.4 %while.19 = (s32[]{:T(128)}, f32[64,2,4]{0,2,1:T(4,128)S(1)}, f32[64,2,4]{0,2,1:T(4,128)S(1)}, f32[64,2,4,64]{3,2,1,0:T(4,128)S(1)}, f32[8,64,2,4]{1,3,2,0:T(4,1...) while((s32[]{:T(128)}, f32[64,2,4]{0,2,1:T(4,128)S(1)}, ...), condition=%wide.region_10.11_spmd, body=%wide.region_9.10_spmd.sunk | while | flops 101381 | bytes 684175 | solution.py:19
  115.2 1.0 constant_dynamic-slice_fusion.2
  117.3 1.0 constant_dynamic-slice_fusion.2
  119.4 1.0 constant_dynamic-slice_fusion.2
  121.4 1.0 constant_dynamic-slice_fusion.2
  123.5 1.0 constant_dynamic-slice_fusion.2
  125.5 1.0 constant_dynamic-slice_fusion.2
  127.6 1.0 constant_dynamic-slice_fusion.2
  131.5 1.3 dynamic-slice
  133.4 74.0 %all-reduce.5.cloned.1.call-done = bf16[32,1024]{1,0:T(8,128)(2,1)} async-done(((bf16[32,1024]{1,0:T(8,128)(2,1)}), bf16[32,1024]{1,0:T(8,128)(2,1)}) %all-reduce.5.cloned.1.call-update) | async-done | bytes 65552
  207.4 0.8 multiply_reduce_fusion
  209.0 48.0 %all-gather.4 = bf16[64,4,1024]{2,1,0:T(4,128)(2,1)S(1)} all-gather(bf16[1,4,1024]{2,1,0:T(4,128)(2,1)S(1)} %fusion.38), channel_id=1, replica_groups=mesh['req'=8,'seq'=8,'tp'=8] {'seq','tp'}, dimensions={0}, use_global_device_ids=true | all-gather | bytes 532480 | tf_op jit(solution)/shard_map/all_gather | solution.py:259
  257.5 1.4 fusion.13
  258.9 1.3 dynamic-slice.2
  260.8 194.3 %all-reduce.7.cloned.1.call-done = f32[256,1024]{1,0:T(8,128)} async-done(((f32[256,1024]{1,0:T(8,128)}), f32[256,1024]{1,0:T(8,128)}) %all-reduce.7.cloned.1.call-update) | async-done | bytes 1048592
  455.2 1.4 fusion.34
  (134 shorter events, 21.2 us)
Async XLA Ops:
  6.5 124.0 %copy-start = (bf16[128,1024]{1,0:T(8,128)(2,1)S(1)}, bf16[128,1024]{1,0:T(8,128)(2,1)}, u32[]{:S(2)}) copy-start(bf16[128,1024]{1,0:T(8,128)(2,1)} %param.18) | copy-start | bytes 786436
  6.5 65.1 %copy-start.4 = (bf16[1024,3,128]{2,0,1:T(8,128)(2,1)S(1)}, bf16[1024,3,128]{2,0,1:T(8,128)(2,1)}, u32[]{:S(2)}) copy-start(bf16[1024,3,128]{2,0,1:T(8,128)(2,1)} %param.17) | copy-start | bytes 2359300
  6.5 107.2 %all-gather.7.cloned.1.call-start = ((), (), s32[]{:S(2)}) async-start(), calls=%async_computation | async-start | bytes 2359296 | tf_op jit(solution)/shard_map/all_gather | solution.py:13
  72.0 2.6 copy-start.1
  72.4 0.8 copy-start.3
  74.5 0.7 copy-start.16
  74.6 0.7 copy-start.17
  74.6 0.8 copy-start.12
  75.3 4.4 copy-start.2
  75.4 2.6 copy-start.10
  79.7 0.7 copy-start.11
  80.5 4.1 copy-start.8
  80.5 4.2 copy-start.7
  83.1 124.3 %all-reduce.5.cloned.1.call-start = ((), (), s32[]{:S(2)}) async-start(), calls=%async_computation.1 | async-start | bytes 131072
  85.5 28.2 %copy-start.13 = (s32[64,4]{0,1:T(4,128)S(1)}, s32[64,4]{0,1:T(4,128)}, u32[]{:S(2)}) copy-start(s32[64,4]{0,1:T(4,128)} %param.27) | copy-start | bytes 3076
  85.5 28.2 %copy-start.14 = (f32[2]{0:T(128)S(1)}, f32[2]{0:T(128)}, u32[]{:S(2)}) copy-start(f32[2]{0:T(128)} %get-tuple-element.258) | copy-start | bytes 28
  129.9 77.5 %copy-start.6 = (bf16[4,1024]{1,0:T(4,128)(2,1)S(1)}, bf16[4,1024]{1,0:T(4,128)(2,1)}, u32[]{:S(2)}) copy-start(bf16[4,1024]{1,0:T(4,128)(2,1)} %param.16) | copy-start | bytes 24580
  129.9 78.3 %copy-start.15 = (f32[1024]{0:T(1024)S(1)}, f32[1024]{0:T(1024)}, u32[]{:S(2)}) copy-start(f32[1024]{0:T(1024)} %param.21) | copy-start | bytes 12292
  130.3 126.9 %copy-start.5 = (bf16[1024,1,128]{2,0,1:T(8,128)(2,1)S(1)}, bf16[1024,1,128]{2,0,1:T(8,128)(2,1)}, u32[]{:S(2)}) copy-start(bf16[1024,1,128]{2,0,1:T(8,128)(2,1)} %param.22) | copy-start | bytes 786436
  130.4 127.1 %copy-start.9 = (bf16[1,64,1024]{2,1,0:T(8,128)(2,1)S(1)}, bf16[1,64,1024]{2,1,0:T(8,128)(2,1)}, u32[]{:S(2)}) copy-start(bf16[1,64,1024]{2,1,0:T(8,128)(2,1)} %param.23) | copy-start | bytes 393220
  131.4 323.8 %all-reduce.7.cloned.1.call-start = ((), (), s32[]{:S(2)}) async-start(), calls=%async_computation.2 | async-start | bytes 2097152
Sparse Core Ops, SparseCore 0:
  83.2 27.9 all-gather.6
  131.5 75.8 all-reduce.4
  259.0 196.1 all-reduce.6
where the time goes:
time: 464 us; the launch traced here: 463 us
  waiting for transfers between devices  268 us (58%)
  blocking collectives  130 us (28%)
  local copies, waits for them, and re-layouts  20.9 us (5%)
  other arithmetic  20.4 us (4%)
  between operations  14.9 us (3%)
  matrix products  7.98 us (2%)
    unnamed x5, waiting for transfers between devices  268 us
    all_gather x1, blocking collectives, on_device(): lax.all_gather(normed, ('seq', 'tp'), axis=0, tiled=True)  55.1 us
    all_gather x1, blocking collectives, on_device(): lax.all_gather(normed_mid, ('seq', 'tp'), axis=0, tiled=True)  48 us
    all_gather x2, blocking collectives, joined(): everything = jax.tree.map(lambda part: lax.all_gather(part, axis), value)  27.1 us
  transfers between devices with their start and end apart: 3, of which 2 were waited for; matrix products, arithmetic and copies ran while one was open for 1% of the time, Pallas kernels for 0%

commit v1 on v0

--- a/solution.py
+++ b/solution.py
@@ -7,6 +7,13 @@
 HD = 64
 EPSILON = 1e-05
 MASKED_SCORE = -1e30
+
+
+def all_by_exchange(block, axis, dim):
+    n_dev = lax.axis_size(axis)
+    tiles = jnp.stack([block for _ in range(n_dev)])
+    tiles = lax.all_to_all(tiles, axis, split_axis=0, concat_axis=0)
+    return jnp.concatenate(tiles, axis=dim)
 
 
 def joined(value, axis, combine):
@@ -209,9 +216,7 @@
     qkv_width = w_qkv.shape[2]
     flat_qkv = w_qkv.reshape(w_qkv.shape[0], 3 * qkv_width)
     projected = jnp.dot(
-        lax.all_gather(normed, ("seq", "tp"), axis=0, tiled=True),
-        flat_qkv,
-        preferred_element_type=jnp.float32,
+        all_by_exchange(normed, ("seq", "tp"), 0), flat_qkv, preferred_element_type=jnp.float32
     )
     queries, keys_new, values_new = split_heads(projected, row_positions(cache_len, step_count), HD)
     shape_four = (requests, step_count, qkv_width // HD, HD)

time: 464 us -> 435 us (0.938)
  blocking collectives: 130 us -> 75.2 us
  starting transfers between devices: 0.09 us -> 13.9 us
  waiting for transfers between devices: 268 us -> 278 us
  local copies, waits for them, and re-layouts: 20.9 us -> 26.2 us
    all_gather x1 -> x0, blocking collectives: 55.1 us -> none  [on_device(): lax.all_gather(normed, ('seq', 'tp'), axis=0, tiled=True)]
    all_to_all x0 -> x1, starting transfers between devices: none -> 13.8 us  [all_by_exchange(): tiles = lax.all_to_all(tiles, axis, split_axis=0, concat_axis=0)]
    all_to_all x0 -> x1, waiting for transfers between devices: none -> 10.1 us  [all_by_exchange(): tiles = lax.all_to_all(tiles, axis, split_axis=0, concat_axis=0)]
  transfers between devices with their start and end apart: 3 -> 4, of which waited for: 2 -> 3; matrix products, arithmetic and copies ran while one was open for 1% -> 3% of each run, Pallas kernels for 0% -> 0%
where the time goes in v1:
time: 435 us; the launch traced here: 434 us
  waiting for transfers between devices  278 us (64%)
  blocking collectives  75.2 us (17%)
  local copies, waits for them, and re-layouts  26.2 us (6%)
  other arithmetic  16.2 us (4%)
  between operations  14.9 us (3%)
  starting transfers between devices  13.9 us (3%)
  matrix products  9.99 us (2%)
    unnamed x5, waiting for transfers between devices  268 us
    all_gather x1, blocking collectives, on_device(): lax.all_gather(normed_mid, ('seq', 'tp'), axis=0, tiled=True)  48 us
    all_gather x2, blocking collectives, joined(): everything = jax.tree.map(lambda part: lax.all_gather(part, axis), value)  27.2 us
    all_to_all x1, starting transfers between devices, all_by_exchange(): tiles = lax.all_to_all(tiles, axis, split_axis=0, concat_axis=0)  13.8 us
    all_to_all x1, waiting for transfers between devices, all_by_exchange(): tiles = lax.all_to_all(tiles, axis, split_axis=0, concat_axis=0)  10.1 us
  transfers between devices with their start and end apart: 4, of which 3 were waited for; matrix products, arithmetic and copies ran while one was open for 3% of the time, Pallas kernels for 0%

profile of v1, /device:TPU:8, one launch (start us, length us, event | category | flops | bytes accessed | tf_op | source)
XLA Modules:
  0.0 434.4 jit_solution(12755849233721052904)
XLA Ops:
  8.2 0.9 stack.2
  9.2 13.8 %all-to-all-start = ((bf16[64,4,1024]{2,1,0:T(4,128)(2,1)}), bf16[64,4,1024]{2,1,0:T(4,128)(2,1)S(1)}, u32[]{:S(2)}, u32[]{:S(2)}) async-start(bf16[64,4,1024]{2,1,0:T(4,128)(2,1)} %stack.2), calls=%async_computation | async-start | bytes 1048576 | tf_op jit(solution)/shard_map/all_to_all | solution.py:15
  25.0 1.7 copy.146
  26.7 2.6 copy.154
  31.0 10.1 %all-to-all-done = bf16[64,4,1024]{2,1,0:T(4,128)(2,1)S(1)} async-done(((bf16[64,4,1024]{2,1,0:T(4,128)(2,1)}), bf16[64,4,1024]{2,1,0:T(4,128)(2,1)S(1)}, u32[]{:S(2)}, u32[]{:S(2)}) %all-to-all-start) | async-done | bytes 524320 | tf_op jit(solution)/shard_map/all_to_all | solution.py:15
  41.0 0.9 reshape.228
  41.9 1.5 fusion.10
  46.1 1.0 copy.145
  47.8 1.0 convolution_convert_fusion.1
  48.9 1.8 fusion.46
  51.0 1.2 fusion.20
  52.4 1.5 convolution_multiply_fusion.1
  53.9 1.0 fusion.22
  55.1 0.9 slice.97
  57.9 13.4 %all-gather = f32[512,2,4]{2,1,0:T(2,128)S(1)} all-gather(f32[64,2,4]{2,1,0:T(2,128)S(1)} %copy.150), channel_id=2, replica_groups=mesh['req'=8,'seq'=8,'tp'=8] {'seq'}, dimensions={0}, use_global_device_ids=true | all-gather | bytes 18432 | tf_op jit(solution)/shard_map/all_gather | solution.py:20
  71.6 13.7 %all-gather.1 = f32[512,2,4]{2,1,0:T(2,128)S(1)} all-gather(f32[64,2,4]{2,1,0:T(2,128)S(1)} %copy.153), channel_id=3, replica_groups=mesh['req'=8,'seq'=8,'tp'=8] {'seq'}, dimensions={0}, use_global_device_ids=true | all-gather | bytes 18432 | tf_op jit(solution)/shard_map/all_gather | solution.py:20
  85.8 1.0 slice.67
  87.0 14.4 %while.19 = (s32[]{:T(128)}, f32[64,2,4]{0,2,1:T(4,128)S(1)}, f32[64,2,4]{0,2,1:T(4,128)S(1)}, f32[64,2,4,64]{3,2,1,0:T(4,128)S(1)}, f32[8,64,2,4]{1,3,2,0:T(4,1...) while((s32[]{:T(128)}, f32[64,2,4]{0,2,1:T(4,128)S(1)}, ...), condition=%wide.region_10.11_spmd, body=%wide.region_9.10_spmd.sunk | while | flops 101381 | bytes 684175 | solution.py:26
  87.3 1.0 constant_dynamic-slice_fusion.2
  89.3 1.0 constant_dynamic-slice_fusion.2
  91.4 1.0 constant_dynamic-slice_fusion.2
  93.5 1.0 constant_dynamic-slice_fusion.2
  95.5 1.0 constant_dynamic-slice_fusion.2
  97.6 1.0 constant_dynamic-slice_fusion.2
  99.6 1.0 constant_dynamic-slice_fusion.2
  103.5 1.3 dynamic-slice
  105.4 73.2 %all-reduce.5.cloned.1.call-done = bf16[32,1024]{1,0:T(8,128)(2,1)} async-done(((bf16[32,1024]{1,0:T(8,128)(2,1)}), bf16[32,1024]{1,0:T(8,128)(2,1)}) %all-reduce.5.cloned.1.call-update) | async-done | bytes 65552
  180.2 48.0 %all-gather.3 = bf16[64,4,1024]{2,1,0:T(4,128)(2,1)S(1)} all-gather(bf16[1,4,1024]{2,1,0:T(4,128)(2,1)S(1)} %fusion.38), channel_id=1, replica_groups=mesh['req'=8,'seq'=8,'tp'=8] {'seq','tp'}, dimensions={0}, use_global_device_ids=true | all-gather | bytes 532480 | tf_op jit(solution)/shard_map/all_gather | solution.py:264
  228.7 1.4 fusion.13
  230.1 1.3 dynamic-slice.2
  232.0 194.5 %all-reduce.7.cloned.1.call-done = f32[256,1024]{1,0:T(8,128)} async-done(((f32[256,1024]{1,0:T(8,128)}), f32[256,1024]{1,0:T(8,128)}) %all-reduce.7.cloned.1.call-update) | async-done | bytes 1048592
  426.5 1.4 fusion.34
  (142 shorter events, 23.5 us)
Async XLA Ops:
  6.5 96.1 %copy-start = (bf16[128,1024]{1,0:T(8,128)(2,1)S(1)}, bf16[128,1024]{1,0:T(8,128)(2,1)}, u32[]{:S(2)}) copy-start(bf16[128,1024]{1,0:T(8,128)(2,1)} %param.18) | copy-start | bytes 786436
  6.5 16.5 %copy-start.13 = (s32[64,64]{1,0:T(8,128)S(1)}, s32[64,64]{1,0:T(8,128)}, u32[]{:S(2)}) copy-start(s32[64,64]{1,0:T(8,128)} %param.28) | copy-start | bytes 49156
  6.5 17.7 %copy-start.19 = (s32[64]{0:T(128)S(1)}, s32[64]{0:T(128)}, u32[]{:S(2)}) copy-start(s32[64]{0:T(128)} %param.29) | copy-start | bytes 772
  6.5 17.8 %copy-start.15 = (s32[64,4]{0,1:T(4,128)S(1)}, s32[64,4]{0,1:T(4,128)}, u32[]{:S(2)}) copy-start(s32[64,4]{0,1:T(4,128)} %param.27) | copy-start | bytes 3076
  6.5 18.1 %copy-start.3 = (bf16[1024,3,128]{2,0,1:T(8,128)(2,1)S(1)}, bf16[1024,3,128]{2,0,1:T(8,128)(2,1)}, u32[]{:S(2)}) copy-start(bf16[1024,3,128]{2,0,1:T(8,128)(2,1)} %param.17) | copy-start | bytes 2359300
  9.2 31.8 %all-to-all-start = ((bf16[64,4,1024]{2,1,0:T(4,128)(2,1)}), bf16[64,4,1024]{2,1,0:T(4,128)(2,1)S(1)}, u32[]{:S(2)}, u32[]{:S(2)}) async-start(bf16[64,4,1024]{2,1,0:T(4,128)(2,1)} %stack.2), calls=%async_computation | async-start | bytes 1048576 | tf_op jit(solution)/shard_map/all_to_all | solution.py:15
  23.0 62.8 %all-gather.6.cloned.1.call-start = ((), (), s32[]{:S(2)}) async-start(), calls=%async_computation.1 | async-start | bytes 2359296 | tf_op jit(solution)/shard_map/all_gather | solution.py:20
  26.7 2.7 copy-start.20
  26.7 3.4 copy-start.14
  43.4 0.7 copy-start.2
  44.8 0.6 copy-start.4
  44.8 0.6 copy-start.6
  44.8 7.5 %copy-start.1 = (bf16[24,256,128]{1,2,0:T(8,128)(2,1)S(1)}, bf16[24,256,128]{1,2,0:T(8,128)(2,1)}, u32[]{:S(2)}) copy-start(bf16[24,256,128]{1,2,0:T(8,128)(2,1)} %copy.154) | copy-start | bytes 4718596
  52.4 3.6 copy-start.7
  52.4 3.7 copy-start.5
  52.4 4.1 copy-start.11
  52.4 4.2 copy-start.10
  55.0 123.6 %all-reduce.5.cloned.1.call-start = ((), (), s32[]{:S(2)}) async-start(), calls=%async_computation.2 | async-start | bytes 131072
  57.4 28.2 %copy-start.16 = (f32[2]{0:T(128)S(1)}, f32[2]{0:T(128)}, u32[]{:S(2)}) copy-start(f32[2]{0:T(128)} %get-tuple-element.257) | copy-start | bytes 28
  57.5 28.2 %copy-start.17 = (f32[2]{0:T(128)S(1)}, f32[2]{0:T(128)}, u32[]{:S(2)}) copy-start(f32[2]{0:T(128)} %get-tuple-element.258) | copy-start | bytes 28
  102.0 76.6 %copy-start.9 = (bf16[4,1024]{1,0:T(4,128)(2,1)S(1)}, bf16[4,1024]{1,0:T(4,128)(2,1)}, u32[]{:S(2)}) copy-start(bf16[4,1024]{1,0:T(4,128)(2,1)} %param.16) | copy-start | bytes 24580
  102.0 77.5 %copy-start.18 = (f32[1024]{0:T(1024)S(1)}, f32[1024]{0:T(1024)}, u32[]{:S(2)}) copy-start(f32[1024]{0:T(1024)} %param.21) | copy-start | bytes 12292
  102.4 126.0 %copy-start.8 = (bf16[1024,1,128]{2,0,1:T(8,128)(2,1)S(1)}, bf16[1024,1,128]{2,0,1:T(8,128)(2,1)}, u32[]{:S(2)}) copy-start(bf16[1024,1,128]{2,0,1:T(8,128)(2,1)} %param.22) | copy-start | bytes 786436
  102.5 126.2 %copy-start.12 = (bf16[1,64,1024]{2,1,0:T(8,128)(2,1)S(1)}, bf16[1,64,1024]{2,1,0:T(8,128)(2,1)}, u32[]{:S(2)}) copy-start(bf16[1,64,1024]{2,1,0:T(8,128)(2,1)} %param.23) | copy-start | bytes 393220
  103.4 323.1 %all-reduce.7.cloned.1.call-start = ((), (), s32[]{:S(2)}) async-start(), calls=%async_computation.3 | async-start | bytes 2097152
Sparse Core Ops, SparseCore 0:
  55.1 27.3 all-gather.5
  103.5 74.9 all-reduce.4
  230.2 196.2 all-reduce.6
